TPU v7x, 32 devices: a whole 2x2x4 slice. The times are simulated.
32 devices in a mesh: dp: 2 (over core), ctx: 16 (over z, y, x).
Axes of the slice: x: 2, y: 2, z: 4, core: 2. Of those that a mesh axis runs over, the one named last changes fastest.
Arguments:
- layer_in: bfloat16 [2, 4096, 768], P('dp', 'ctx'), may hold values from -6 to 6
- out_grad: bfloat16 [2, 4096, 768], P('dp', 'ctx'), may hold values from -6 to 6
- first_gain: bfloat16 [768], P('dp'), may hold values from 0.099609375 to 1.8984375
- query_weight: bfloat16 [768, 768], P('dp'), may hold values from -0.21875 to 0.21875
- key_weight: bfloat16 [768, 768], P('dp'), may hold values from -0.21875 to 0.21875
- value_weight: bfloat16 [768, 768], P('dp'), may hold values from -0.21875 to 0.21875
- output_weight: bfloat16 [768, 768], P('dp'), may hold values from -6 to 6
- second_gain: bfloat16 [768], P('dp'), may hold values from 0.099609375 to 1.8984375
- gate_weight: bfloat16 [768, 2048], P('dp'), may hold values from -0.21875 to 0.21875
- up_weight: bfloat16 [768, 2048], P('dp'), may hold values from -0.21875 to 0.21875
- down_weight: bfloat16 [2048, 768], P('dp'), may hold values from -0.125 to 0.125
Outputs:
- layer_out: bfloat16 [2, 4096, 768], P('dp', 'ctx')
- in_grad: bfloat16 [2, 4096, 768], P('dp', 'ctx')
- first_gain_grad: float32 [768], P('dp')
- query_grad: float32 [768, 768], P('dp')
- key_grad: float32 [768, 768], P('dp')
- value_grad: float32 [768, 768], P('dp')
- output_grad: float32 [768, 768], P('dp')
- second_gain_grad: float32 [768], P('dp')
- gate_grad: float32 [768, 2048], P('dp')
- up_grad: float32 [768, 2048], P('dp')
- down_grad: float32 [2048, 768], P('dp')
All inputs are finite; a program needn't handle non-finite values.
Results may differ from a plain program's by a relative error of at most 0.02.
Values may be sent and summed in bfloat16 or wider, within the bound.
No kernel may reach another device: no remote copies, remote signals or barrier semaphores. Data moves between devices by JAX's collectives and lax.ppermute only.
A program may use at most 448 MiB of HBM per device.

v0:
```python
import jax
import jax.numpy as jnp
from jax import lax
from jax.sharding import PartitionSpec as P

HEADS = 12
HEAD_DIM = 64
EPS = 1e-06


def normed(rows, gain):
    return rows * lax.rsqrt(jnp.mean(rows * rows, axis=-1, keepdims=True) + EPS) * gain


def gated(gate, upper):
    return jax.nn.gelu(gate, approximate=True) * upper


def heads_of(rows):
    return rows.reshape(rows.shape[0], HEADS, HEAD_DIM)


def scores_of(query, keys):
    return jnp.einsum(
        "qhd,khd->hqk", heads_of(query), heads_of(keys), preferred_element_type=jnp.float32
    ) * HEAD_DIM ** (-0.5)


def attend(operands):
    query, keys, values = operands
    scores = scores_of(query, keys)
    top = jnp.max(scores, axis=-1, keepdims=True)
    expd = jnp.exp(scores - top)
    total = jnp.sum(expd, axis=-1, keepdims=True)
    probs = (expd / total).astype(jnp.bfloat16)
    mixed = jnp.einsum("hqk,khd->qhd", probs, heads_of(values), preferred_element_type=jnp.float32)
    mixed = mixed.reshape(query.shape[0], HEADS * HEAD_DIM).astype(jnp.bfloat16)
    return (mixed, (top + jnp.log(total))[..., 0])


def back_core(query, keys, values, grad_mix, logsum):
    probs = jnp.exp(scores_of(query, keys) - logsum[..., None])
    grad_prob = jnp.einsum(
        "qhd,khd->hqk", heads_of(grad_mix), heads_of(values), preferred_element_type=jnp.float32
    )
    delta = jnp.sum(grad_prob * probs, axis=-1)
    grad_score = (probs * (grad_prob - delta[..., None])).astype(jnp.bfloat16)
    return (probs, grad_score, delta)


def query_part(grad_score, keys, count):
    grad_query = jnp.einsum(
        "hqk,khd->qhd", grad_score, heads_of(keys), preferred_element_type=jnp.float32
    ) * HEAD_DIM ** (-0.5)
    return grad_query.reshape(count, HEADS * HEAD_DIM).astype(jnp.bfloat16)


def attend_back(operands):
    query, keys, values, grad_mix, logsum = operands
    probs, grad_score, delta = back_core(query, keys, values, grad_mix, logsum)
    grad_query = query_part(grad_score, keys, query.shape[0])
    grad_keys = jnp.einsum(
        "hqk,qhd->khd", grad_score, heads_of(query), preferred_element_type=jnp.float32
    ) * HEAD_DIM ** (-0.5)
    grad_values = jnp.einsum(
        "hqk,qhd->khd",
        probs.astype(jnp.bfloat16),
        heads_of(grad_mix),
        preferred_element_type=jnp.float32,
    )
    return (
        grad_query,
        grad_keys.reshape(keys.shape[0], -1),
        grad_values.reshape(keys.shape[0], -1),
    )


def product(left, right):
    return jnp.dot(left, right, preferred_element_type=jnp.float32)


def on_device(
    layer_in,
    out_grad,
    first_gain,
    query_weight,
    key_weight,
    value_weight,
    output_weight,
    second_gain,
    gate_weight,
    up_weight,
    down_weight,
):
    seqs, local, width = layer_in.shape
    rows = seqs * local

    def shaped(matrix):
        return matrix.reshape(seqs, local, width)

    gain_one, w_query, w_key, w_value, w_output = (
        lax.all_gather(first_gain, "dp", axis=0, tiled=True),
        lax.all_gather(query_weight, "dp", axis=0, tiled=True),
        lax.all_gather(key_weight, "dp", axis=0, tiled=True),
        lax.all_gather(value_weight, "dp", axis=0, tiled=True),
        lax.all_gather(output_weight, "dp", axis=0, tiled=True),
    )
    inputs = layer_in.reshape(rows, width).astype(jnp.float32)
    gain_one_f = gain_one.astype(jnp.float32)
    normal_one = normed(inputs, gain_one_f).astype(jnp.bfloat16)
    query = product(normal_one, w_query).astype(jnp.bfloat16)
    keys = product(normal_one, w_key).astype(jnp.bfloat16)
    values = product(normal_one, w_value).astype(jnp.bfloat16)
    keys_all, values_all = (
        lax.all_gather(shaped(keys), "ctx", axis=1, tiled=True),
        lax.all_gather(shaped(values), "ctx", axis=1, tiled=True),
    )
    mixed, logsum = lax.map(attend, (shaped(query), keys_all, values_all))
    mixed_rows = mixed.reshape(rows, width)
    middle = inputs + product(mixed_rows, w_output)
    gain_two, w_gate, w_up, w_down = (
        lax.all_gather(second_gain, "dp", axis=0, tiled=True),
        lax.all_gather(gate_weight, "dp", axis=0, tiled=True),
        lax.all_gather(up_weight, "dp", axis=0, tiled=True),
        lax.all_gather(down_weight, "dp", axis=0, tiled=True),
    )
    gain_two_f = gain_two.astype(jnp.float32)
    normal_two = normed(middle, gain_two_f).astype(jnp.bfloat16)
    gate = product(normal_two, w_gate)
    upper = product(normal_two, w_up)
    hidden = gated(gate, upper).astype(jnp.bfloat16)
    result = middle + product(hidden, w_down)
    layer_out = result.astype(jnp.bfloat16).reshape(seqs, local, width)
    gain_one, w_query, w_key, w_value, w_output = (
        lax.all_gather(first_gain, "dp", axis=0, tiled=True),
        lax.all_gather(query_weight, "dp", axis=0, tiled=True),
        lax.all_gather(key_weight, "dp", axis=0, tiled=True),
        lax.all_gather(value_weight, "dp", axis=0, tiled=True),
        lax.all_gather(output_weight, "dp", axis=0, tiled=True),
    )
    gain_two, w_gate, w_up, w_down = (
        lax.all_gather(second_gain, "dp", axis=0, tiled=True),
        lax.all_gather(gate_weight, "dp", axis=0, tiled=True),
        lax.all_gather(up_weight, "dp", axis=0, tiled=True),
        lax.all_gather(down_weight, "dp", axis=0, tiled=True),
    )
    gain_one_f = gain_one.astype(jnp.float32)
    gain_two_f = gain_two.astype(jnp.float32)
    grad_rows = out_grad.reshape(rows, width)
    grad_down = product(hidden.T, grad_rows)
    grad_hidden = product(grad_rows, w_down.T)
    unused, gate_back = jax.vjp(gated, gate, upper)
    grad_gate, grad_upper = gate_back(grad_hidden)
    grad_gate = grad_gate.astype(jnp.bfloat16)
    grad_upper = grad_upper.astype(jnp.bfloat16)
    grad_wgate = product(normal_two.T, grad_gate)
    grad_wup = product(normal_two.T, grad_upper)
    grad_normal_two = product(grad_gate, w_gate.T) + product(grad_upper, w_up.T)
    unused_two, norm_back_two = jax.vjp(normed, middle, gain_two_f)
    grad_middle, grad_gain_two = norm_back_two(grad_normal_two)
    grad_middle = grad_middle + grad_rows.astype(jnp.float32)
    ffn_terms = (
        lax.psum_scatter(
            grad_gain_two.astype(jnp.bfloat16), "dp", scatter_dimension=0, tiled=True
        ).astype(jnp.float32),
        lax.psum_scatter(
            grad_wgate.astype(jnp.bfloat16), "dp", scatter_dimension=0, tiled=True
        ).astype(jnp.float32),
        lax.psum_scatter(
            grad_wup.astype(jnp.bfloat16), "dp", scatter_dimension=0, tiled=True
        ).astype(jnp.float32),
        lax.psum_scatter(
            grad_down.astype(jnp.bfloat16), "dp", scatter_dimension=0, tiled=True
        ).astype(jnp.float32),
    )
    ffn_total = (
        lax.psum(ffn_terms[0].astype(jnp.bfloat16), "ctx").astype(jnp.float32),
        lax.psum(ffn_terms[1].astype(jnp.bfloat16), "ctx").astype(jnp.float32),
        lax.psum(ffn_terms[2].astype(jnp.bfloat16), "ctx").astype(jnp.float32),
        lax.psum(ffn_terms[3].astype(jnp.bfloat16), "ctx").astype(jnp.float32),
    )
    grad_branch = grad_middle.astype(jnp.bfloat16)
    grad_woutput = product(mixed_rows.T, grad_branch)
    grad_mixed = product(grad_branch, w_output.T).astype(jnp.bfloat16)
    grad_query, grad_keys_all, grad_values_all = lax.map(
        attend_back, (shaped(query), keys_all, values_all, shaped(grad_mixed), logsum)
    )
    grad_keys, grad_values = (
        lax.psum_scatter(
            grad_keys_all.astype(jnp.bfloat16), "ctx", scatter_dimension=1, tiled=True
        ).astype(jnp.float32),
        lax.psum_scatter(
            grad_values_all.astype(jnp.bfloat16), "ctx", scatter_dimension=1, tiled=True
        ).astype(jnp.float32),
    )
    grad_keys = grad_keys.astype(jnp.bfloat16)
    grad_values = grad_values.astype(jnp.bfloat16)
    grad_query = grad_query.reshape(rows, width)
    grad_keys = grad_keys.reshape(rows, width)
    grad_values = grad_values.reshape(rows, width)
    grad_wquery = product(normal_one.T, grad_query)
    grad_wkey = product(normal_one.T, grad_keys)
    grad_wvalue = product(normal_one.T, grad_values)
    grad_normal_one = (
        product(grad_query, w_query.T)
        + product(grad_keys, w_key.T)
        + product(grad_values, w_value.T)
    )
    unused_one, norm_back_one = jax.vjp(normed, inputs, gain_one_f)
    grad_inputs, grad_gain_one = norm_back_one(grad_normal_one)
    in_grad = (grad_inputs + grad_middle).astype(jnp.bfloat16).reshape(seqs, local, width)
    attn_terms = (
        lax.psum_scatter(
            grad_gain_one.astype(jnp.bfloat16), "dp", scatter_dimension=0, tiled=True
        ).astype(jnp.float32),
        lax.psum_scatter(
            grad_wquery.astype(jnp.bfloat16), "dp", scatter_dimension=0, tiled=True
        ).astype(jnp.float32),
        lax.psum_scatter(
            grad_wkey.astype(jnp.bfloat16), "dp", scatter_dimension=0, tiled=True
        ).astype(jnp.float32),
        lax.psum_scatter(
            grad_wvalue.astype(jnp.bfloat16), "dp", scatter_dimension=0, tiled=True
        ).astype(jnp.float32),
        lax.psum_scatter(
            grad_woutput.astype(jnp.bfloat16), "dp", scatter_dimension=0, tiled=True
        ).astype(jnp.float32),
    )
    attn_total = (
        lax.psum(attn_terms[0].astype(jnp.bfloat16), "ctx").astype(jnp.float32),
        lax.psum(attn_terms[1].astype(jnp.bfloat16), "ctx").astype(jnp.float32),
        lax.psum(attn_terms[2].astype(jnp.bfloat16), "ctx").astype(jnp.float32),
        lax.psum(attn_terms[3].astype(jnp.bfloat16), "ctx").astype(jnp.float32),
        lax.psum(attn_terms[4].astype(jnp.bfloat16), "ctx").astype(jnp.float32),
    )
    return (
        layer_out,
        in_grad,
        attn_total[0],
        attn_total[1],
        attn_total[2],
        attn_total[3],
        attn_total[4],
        ffn_total[0],
        ffn_total[1],
        ffn_total[2],
        ffn_total[3],
    )


def solution(mesh):
    in_specs = (
        P("dp", "ctx", None),
        P("dp", "ctx", None),
        P("dp"),
        P("dp", None),
        P("dp", None),
        P("dp", None),
        P("dp", None),
        P("dp"),
        P("dp", None),
        P("dp", None),
        P("dp", None),
    )
    out_specs = (
        P("dp", "ctx", None),
        P("dp", "ctx", None),
        P("dp"),
        P("dp", None),
        P("dp", None),
        P("dp", None),
        P("dp", None),
        P("dp"),
        P("dp", None),
        P("dp", None),
        P("dp", None),
    )
    return jax.shard_map(
        on_device, mesh=mesh, in_specs=in_specs, out_specs=out_specs, check_vma=False
    )
```

profile of v0, /device:TPU:0, one launch (start us, length us, event | category | flops | bytes accessed | tf_op | source)
XLA Modules:
  0.0 1049.3 jit_solution(17920821551046934564)
XLA Ops:
  10.1 1.9 all-gather.2
  13.8 7.7 all-gather.18.cloned.1.call-done
  21.5 2.7 convolution_convert_fusion.8
  24.3 9.2 all-gather.14.cloned.1.call-done
  33.5 2.5 convolution_convert_fusion.10
  40.8 4.7 all-gather.16.cloned.1.call-done
  45.5 1.8 convolution_convert_fusion.9
  47.5 96.6 %all-gather.30.cloned.1.call-done = bf16[4096,768]{1,0:T(8,128)(2,1)} async-done(((bf16[256,768]{1,0:T(8,128)(2,1)}), bf16[4096,768]{1,0:T(8,128)(2,1)}) %all-gather.30.cloned.1.call-update) | async-done | bytes 6291472 | tf_op jit(solution)/shard_map/all_gather | solution.py:115
  144.0 8.7 copy.36
  152.7 22.9 %multiply_reduce_fusion.1 = (f32[12,256]{1,0:T(8,128)S(1)}, f32[12,256,4096]{2,1,0:T(8,128)}) fusion(bf16[256,12,64]{0,2,1:T(8,128)(2,1)S(1)} %bitcast.127, bf16[4096,12,64]{0,2,1:T(8,128)(2,1)} %bitcast.119), kind=kOutput, calls=%fused_computation.6 | convolution fusion | flops 1635775488 | bytes 57028608 | tf_op jit(solution)/shard_map/while/body/eval_jaxpr/qhd,khd->hqk/dot_general | solution.py:24
  175.7 20.5 %fusion = f32[12,256]{1,0:T(8,128)S(1)} fusion(f32[12,256,4096]{2,1,0:T(8,128)} %get-tuple-element.75, f32[12,256]{1,0:T(8,128)S(1)} %get-tuple-element.74), kind=kLoop, calls=%fused_computation.5 | loop fusion | flops 37745664 | bytes 50356224 | tf_op jit(solution)/shard_map/while/body/eval_jaxpr/reduce_sum | solution.py:34
  196.2 43.5 %all-gather.28.cloned.1.call-done = bf16[4096,768]{1,0:T(8,128)(2,1)} async-done(((bf16[256,768]{1,0:T(8,128)(2,1)}), bf16[4096,768]{1,0:T(8,128)(2,1)}) %all-gather.28.cloned.1.call-update) | async-done | bytes 6291472 | tf_op jit(solution)/shard_map/all_gather | solution.py:116
  239.7 8.7 copy.34
  248.4 22.0 %fusion.19 = bf16[12,64,256]{2,1,0:T(8,128)(2,1)S(1)} fusion(bf16[4096,12,64]{0,2,1:T(8,128)(2,1)} %bitcast.121, f32[12,256,4096]{2,1,0:T(8,128)} %get-tuple-element.75, f32[12,256]{1,0:T(8,128)S(1)} %fusion, f32[12,256]{1,0:T(8,128)S(1)} %get-tuple-element.74), kind=kOutput, calls=%fused_computation.45 | convolution fusion | flops 1661140992 | bytes 57040896 | tf_op jit(solution)/shard_map/while/body/eval_jaxpr/hqk,khd->qhd/dot_general | solution.py:36
  270.5 1.9 multiply_reduce_fusion.4
  272.6 4.6 fusion.57
  278.5 4.2 fusion.58
  282.7 10.7 %all-gather.26.cloned.1.call-done = bf16[2048,768]{1,0:T(8,128)(2,1)} async-done(((bf16[1024,768]{1,0:T(8,128)(2,1)}), bf16[2048,768]{1,0:T(8,128)(2,1)}) %all-gather.26.cloned.1.call-update) | async-done | bytes 3145744 | tf_op jit(solution)/shard_map/all_gather | solution.py:125
  293.3 6.9 multiply_convert_fusion.2
  305.6 35.5 %multiply_reduce_fusion = (f32[12,256]{1,0:T(8,128)}, f32[12,256,4096]{2,1,0:T(8,128)}) fusion(f32[12,256,4096]{2,1,0:T(8,128)} %get-tuple-element.75, f32[12,256]{1,0:T(8,128)S(1)} %log_add_fusion, bf16[256,12,64]{0,2,1:T(8,128)(2,1)S(1)} %bitcast.125, bf16[4096,12,64]{0,2,1:T(8,128)(2,1)} %bitcast.122), kind=kOutput, calls=%fused_computation.1 | convolution fusion | flops 1660941312 | bytes 107372544 | tf_op jit(solution)/shard_map/while/body/eval_jaxpr/qhd,khd->hqk/dot_general | solution.py:43
  341.1 40.2 %multiply_convert_fusion = bf16[12,256,4096]{2,1,0:T(8,128)(2,1)} fusion(f32[12,256,4096]{2,1,0:T(8,128)} %get-tuple-element.80, f32[12,256,4096]{2,1,0:T(8,128)} %get-tuple-element.75, f32[12,256]{1,0:T(8,128)} %get-tuple-element.79, f32[12,256]{1,0:T(8,128)S(1)} %log_add_fusion), kind=kLoop, calls=%fused_computation | loop fusion | flops 62914560 | bytes 125853696 | tf_op jit(solution)/shard_map/while/body/eval_jaxpr/convert_element_type | solution.py:47
  381.3 15.2 %multiply_convert_fusion.1 = bf16[12,64,4096]{2,1,0:T(8,128)(2,1)} fusion(bf16[256,12,64]{0,2,1:T(8,128)(2,1)S(1)} %bitcast.128, bf16[12,256,4096]{2,1,0:T(8,128)(2,1)} %multiply_convert_fusion), kind=kOutput, calls=%fused_computation.12 | convolution fusion | flops 1616904192 | bytes 31850496 | tf_op jit(solution)/shard_map/while/body/eval_jaxpr/hqk,qhd->khd/dot_general | solution.py:62
  396.6 22.0 %fusion.7 = bf16[12,64,4096]{2,1,0:T(8,128)(2,1)} fusion(bf16[256,12,64]{0,2,1:T(8,128)(2,1)S(1)} %bitcast.126, f32[12,256,4096]{2,1,0:T(8,128)} %get-tuple-element.75, f32[12,256]{1,0:T(8,128)S(1)} %log_add_fusion), kind=kOutput, calls=%fused_computation.13 | convolution fusion | flops 1651507200 | bytes 57028608 | tf_op jit(solution)/shard_map/while/body/eval_jaxpr/hqk,qhd->khd/dot_general | solution.py:65
  418.6 14.4 %fusion.18 = bf16[12,64,256]{2,1,0:T(8,128)(2,1)S(1)} fusion(bf16[4096,12,64]{0,2,1:T(8,128)(2,1)} %bitcast.120, bf16[12,256,4096]{2,1,0:T(8,128)(2,1)} %multiply_convert_fusion), kind=kOutput, calls=%fused_computation.44 | convolution fusion | flops 1611005952 | bytes 31850496 | tf_op jit(solution)/shard_map/while/body/eval_jaxpr/hqk,khd->qhd/dot_general | solution.py:52
  436.4 3.9 convolution_convert_fusion.2
  441.5 2.7 convolution_convert_fusion.1
  445.6 2.7 convolution_convert_fusion
  448.3 95.9 %reduce-scatter.10.cloned.1.call-done = bf16[1,256,768]{1,2,0:T(8,128)(2,1)} async-done(((bf16[1,4096,768]{1,2,0:T(8,128)(2,1)}), bf16[1,256,768]{1,2,0:T(8,128)(2,1)}) %reduce-scatter.10.cloned.1.call-update) | async-done | bytes 393232 | tf_op jit(solution)/shard_map/reduce_scatter | solution.py:189
  544.2 2.6 convolution_convert_fusion.5
  546.9 148.6 %reduce-scatter.12.cloned.1.call-done = bf16[1,256,768]{1,2,0:T(8,128)(2,1)} async-done(((bf16[1,4096,768]{1,2,0:T(8,128)(2,1)}), bf16[1,256,768]{1,2,0:T(8,128)(2,1)}) %reduce-scatter.12.cloned.1.call-update) | async-done | bytes 393232 | tf_op jit(solution)/shard_map/reduce_scatter | solution.py:192
  695.5 2.6 convolution_convert_fusion.4
  698.4 7.6 reduce-scatter.14.cloned.1.call-done
  706.0 12.8 %reduce-scatter.20.cloned.1.call-done = bf16[384,768]{1,0:T(8,128)(2,1)} async-done(((bf16[768,768]{1,0:T(8,128)(2,1)}), bf16[384,768]{1,0:T(8,128)(2,1)}) %reduce-scatter.20.cloned.1.call-update) | async-done | bytes 589840 | tf_op jit(solution)/shard_map/reduce_scatter | solution.py:225
  718.8 14.8 %reduce-scatter.22.cloned.1.call-done = bf16[384,2048]{1,0:T(8,128)(2,1)} async-done(((bf16[768,2048]{1,0:T(8,128)(2,1)}), bf16[384,2048]{1,0:T(8,128)(2,1)}) %reduce-scatter.22.cloned.1.call-update) | async-done | bytes 1572880 | tf_op jit(solution)/shard_map/reduce_scatter | solution.py:166
  733.6 14.9 %reduce-scatter.24.cloned.1.call-done = bf16[384,2048]{1,0:T(8,128)(2,1)} async-done(((bf16[768,2048]{1,0:T(8,128)(2,1)}), bf16[384,2048]{1,0:T(8,128)(2,1)}) %reduce-scatter.24.cloned.1.call-update) | async-done | bytes 1572880 | tf_op jit(solution)/shard_map/reduce_scatter | solution.py:169
  748.4 14.8 %reduce-scatter.26.cloned.1.call-done = bf16[1024,768]{1,0:T(8,128)(2,1)} async-done(((bf16[2048,768]{1,0:T(8,128)(2,1)}), bf16[1024,768]{1,0:T(8,128)(2,1)}) %reduce-scatter.26.cloned.1.call-update) | async-done | bytes 1572880 | tf_op jit(solution)/shard_map/reduce_scatter | solution.py:172
  763.2 12.6 %reduce-scatter.16.cloned.1.call-done = bf16[384,768]{1,0:T(8,128)(2,1)} async-done(((bf16[768,768]{1,0:T(8,128)(2,1)}), bf16[384,768]{1,0:T(8,128)(2,1)}) %reduce-scatter.16.cloned.1.call-update) | async-done | bytes 589840 | tf_op jit(solution)/shard_map/reduce_scatter | solution.py:219
  775.8 12.6 %reduce-scatter.18.cloned.1.call-done = bf16[384,768]{1,0:T(8,128)(2,1)} async-done(((bf16[768,768]{1,0:T(8,128)(2,1)}), bf16[384,768]{1,0:T(8,128)(2,1)}) %reduce-scatter.18.cloned.1.call-update) | async-done | bytes 589840 | tf_op jit(solution)/shard_map/reduce_scatter | solution.py:222
  790.3 1.8 fusion.60
  792.1 3.8 fusion.20
  797.1 2.5 all-reduce.4
  799.8 43.9 %all-reduce.2 = (bf16[384]{0:T(512)(128)(2,1)S(1)}, bf16[384]{0:T(512)(128)(2,1)S(1)}) all-reduce(bf16[384]{0:T(512)(128)(2,1)S(1)} %dynamic-slice.3, bf16[384]{0:T(512)(128)(2,1)S(1)} %dynamic-slice.5), channel_id=1, replica_groups=mesh['dp'=2,'ctx'=16] {'ctx'}, use_global_device_ids=true, to_apply=%region_11.12 | all-reduce | flops 768 | bytes 3072 | tf_op jit(solution)/shard_map/psum | solution.py:230
  845.9 184.0 %all-reduce.7.cloned.1.call-done = (bf16[384,768]{1,0:T(8,128)(2,1)}, bf16[384,768]{1,0:T(8,128)(2,1)}, bf16[384,768]{1,0:T(8,128)(2,1)}, bf16[384,768]{1,0:T(8,...) async-done(((bf16[384,768]{1,0:T(8,128)(2,1)}, bf16[384,768]{1,0:T(8,128)(2,1)}, bf16[384,768]{1,0:T(8,128)(2,1)}, ...) | async-done | bytes 7077904 | tf_op jit(solution)/shard_map/psum | solution.py:231
  1029.9 2.3 convert_element_type.247
  1032.2 2.2 convert_element_type.249
  1036.5 2.0 convert_element_type.257
  1038.6 2.0 convert_element_type.259
  1040.6 1.9 convert_element_type.261
  (137 shorter events, 29.6 us)
Async XLA Ops:
  7.2 26.3 %copy-start = (bf16[1,256,768]{2,1,0:T(8,128)(2,1)S(1)}, bf16[1,256,768]{2,1,0:T(8,128)(2,1)}, u32[]{:S(2)}) copy-start(bf16[1,256,768]{2,1,0:T(8,128)(2,1)} %param.11) | copy-start | bytes 1179652
  7.2 14.3 %all-gather.18.cloned.1.call-start = ((), (), s32[]{:S(2)}) async-start(), calls=%async_computation.11 | async-start | bytes 1769472 | tf_op jit(solution)/shard_map/all_gather | solution.py:104
  7.9 25.6 %all-gather.14.cloned.1.call-start = ((), (), s32[]{:S(2)}) async-start(), calls=%async_computation.9 | async-start | bytes 1769472 | tf_op jit(solution)/shard_map/all_gather | solution.py:105
  8.7 36.8 %all-gather.16.cloned.1.call-start = ((), (), s32[]{:S(2)}) async-start(), calls=%async_computation.10 | async-start | bytes 1769472 | tf_op jit(solution)/shard_map/all_gather | solution.py:103
  9.4 134.6 %all-gather.30.cloned.1.call-start = ((), (), s32[]{:S(2)}) async-start(), calls=%async_computation.26 | async-start | bytes 6684672 | tf_op jit(solution)/shard_map/all_gather | solution.py:115
  12.1 33.4 %copy-start.23 = (f32[768]{0:T(1024)}, f32[768]{0:T(1024)S(1)}, u32[]{:S(2)}) copy-start(f32[768]{0:T(1024)S(1)} %reshape.240) | copy-start | bytes 9220
  13.8 31.6 %copy-start.25 = (f32[256]{0:T(256)}, f32[256]{0:T(256)S(1)}, u32[]{:S(2)}) copy-start(f32[256]{0:T(256)S(1)} %fusion.47) | copy-start | bytes 3076
  24.2 215.5 %all-gather.28.cloned.1.call-start = ((), (), s32[]{:S(2)}) async-start(), calls=%async_computation.25 | async-start | bytes 6684672 | tf_op jit(solution)/shard_map/all_gather | solution.py:116
  36.0 2.9 copy-start.30
  36.1 234.4 %all-gather.20.cloned.1.call-start = ((), (), s32[]{:S(2)}) async-start(), calls=%async_computation.12 | async-start | bytes 1769472 | tf_op jit(solution)/shard_map/all_gather | solution.py:106
  36.6 235.9 %all-gather.22.cloned.1.call-start = ((), (), s32[]{:S(2)}) async-start(), calls=%async_computation.13 | async-start | bytes 4718592 | tf_op jit(solution)/shard_map/all_gather | solution.py:123
  37.4 241.1 %all-gather.24.cloned.1.call-start = ((), (), s32[]{:S(2)}) async-start(), calls=%async_computation.14 | async-start | bytes 4718592 | tf_op jit(solution)/shard_map/all_gather | solution.py:124
  38.1 255.2 %all-gather.26.cloned.1.call-start = ((), (), s32[]{:S(2)}) async-start(), calls=%async_computation.15 | async-start | bytes 4718592 | tf_op jit(solution)/shard_map/all_gather | solution.py:125
  38.9 505.3 %reduce-scatter.10.cloned.1.call-start = ((), (), s32[]{:S(2)}) async-start(), calls=%async_computation.16 | async-start | bytes 6684672 | tf_op jit(solution)/shard_map/reduce_scatter | solution.py:189
  47.4 105.3 %copy-start.3 = (bf16[256,768]{0,1:T(8,128)(2,1)}, bf16[256,768]{0,1:T(8,128)(2,1)S(1)}, u32[]{:S(2)}) copy-start(bf16[256,768]{0,1:T(8,128)(2,1)S(1)} %copy.35) | copy-start | bytes 1179652
  277.2 16.1 %copy-start.11 = (bf16[1,256,768]{2,1,0:T(8,128)(2,1)S(1)}, bf16[1,256,768]{2,1,0:T(8,128)(2,1)}, u32[]{:S(2)}) copy-start(bf16[1,256,768]{2,1,0:T(8,128)(2,1)} %param.12) | copy-start | bytes 1179652
  293.3 7.0 copy-start.10
  300.3 4.4 copy-start.5
  300.3 4.4 copy-start.20
  300.3 2.6 copy-start.1
  302.9 2.0 copy-start.2
  341.1 40.2 %copy-start.4 = (bf16[256,768]{0,1:T(8,128)(2,1)S(1)}, bf16[256,768]{0,1:T(8,128)(2,1)}, u32[]{:S(2)}) copy-start(bf16[256,768]{0,1:T(8,128)(2,1)} %copy-done.3) | copy-start | bytes 1179652
  396.5 299.0 %reduce-scatter.12.cloned.1.call-start = ((), (), s32[]{:S(2)}) async-start(), calls=%async_computation.17 | async-start | bytes 6684672 | tf_op jit(solution)/shard_map/reduce_scatter | solution.py:192
  418.6 14.5 %copy-start.24 = (f32[768]{0:T(1024)S(1)}, f32[768]{0:T(1024)}, u32[]{:S(2)}) copy-start(f32[768]{0:T(1024)} %copy-done.23) | copy-start | bytes 9220
  418.6 14.5 %copy-start.26 = (f32[256]{0:T(256)S(1)}, f32[256]{0:T(256)}, u32[]{:S(2)}) copy-start(f32[256]{0:T(256)} %copy-done.25) | copy-start | bytes 3076
  418.6 287.4 %reduce-scatter.14.cloned.1.call-start = ((), (), s32[]{:S(2)}) async-start(), calls=%async_computation.18 | async-start | bytes 1769472 | tf_op jit(solution)/shard_map/reduce_scatter | solution.py:216
  433.1 3.2 copy-start.7
  434.7 284.0 %reduce-scatter.20.cloned.1.call-start = ((), (), s32[]{:S(2)}) async-start(), calls=%async_computation.21 | async-start | bytes 1769472 | tf_op jit(solution)/shard_map/reduce_scatter | solution.py:225
  436.3 297.2 %reduce-scatter.22.cloned.1.call-start = ((), (), s32[]{:S(2)}) async-start(), calls=%async_computation.22 | async-start | bytes 4718592 | tf_op jit(solution)/shard_map/reduce_scatter | solution.py:166
  440.3 308.1 %reduce-scatter.24.cloned.1.call-start = ((), (), s32[]{:S(2)}) async-start(), calls=%async_computation.23 | async-start | bytes 4718592 | tf_op jit(solution)/shard_map/reduce_scatter | solution.py:169
  444.2 1.3 copy-start.9
  444.2 1.4 copy-start.12
  444.2 318.9 %reduce-scatter.26.cloned.1.call-start = ((), (), s32[]{:S(2)}) async-start(), calls=%async_computation.24 | async-start | bytes 4718592 | tf_op jit(solution)/shard_map/reduce_scatter | solution.py:172
  448.3 327.5 %reduce-scatter.16.cloned.1.call-start = ((), (), s32[]{:S(2)}) async-start(), calls=%async_computation.19 | async-start | bytes 1769472 | tf_op jit(solution)/shard_map/reduce_scatter | solution.py:219
  546.8 241.5 %reduce-scatter.18.cloned.1.call-start = ((), (), s32[]{:S(2)}) async-start(), calls=%async_computation.20 | async-start | bytes 1769472 | tf_op jit(solution)/shard_map/reduce_scatter | solution.py:222
  698.1 331.8 %all-reduce.7.cloned.1.call-start = ((), (), s32[]{:S(2)}) async-start(), calls=%async_computation.27 | async-start | bytes 14155776 | tf_op jit(solution)/shard_map/psum | solution.py:231
  788.4 1.9 copy-start.8
  792.1 3.8 copy-start.13
  792.1 3.8 copy-start.18
  792.1 4.3 copy-start.14
  792.1 4.3 copy-start.19
  795.9 1.3 copy-start.29
  795.9 49.0 %copy-start.28 = (f32[256]{0:T(256)S(1)}, f32[256]{0:T(256)}, u32[]{:S(2)}) copy-start(f32[256]{0:T(256)} %copy-done.27) | copy-start | bytes 3076
  1029.9 4.5 copy-start.22
  1029.9 5.6 copy-start.21
  1029.9 6.7 copy-start.17
  1035.4 3.1 copy-start.16
  1038.6 2.0 copy-start.15
  (3 other events, 2.5 us)
Sparse Core Ops, SparseCore 0:
  9.6 11.9 all-gather.17
  23.1 10.3 all-gather.13
  35.0 10.3 all-gather.15
  48.7 95.2 all-gather.29
  147.2 92.4 all-gather.27
  241.1 7.4 all-gather.19
  250.2 13.2 all-gather.21
  265.0 13.3 all-gather.23
  280.0 13.2 all-gather.25
  396.6 147.5 reduce-scatter.9
  549.4 146.0 reduce-scatter.11
  698.1 7.7 reduce-scatter.13
  708.9 9.8 reduce-scatter.19
  721.4 12.0 reduce-scatter.21
  736.3 12.0 reduce-scatter.23
  751.1 12.0 reduce-scatter.25
  765.9 9.8 reduce-scatter.15
  778.5 9.8 reduce-scatter.17
  795.9 233.8 all-reduce.6
where the time goes:
time: 1060 us; the launch traced here: 1050 us
  waiting for transfers between devices  697 us (66%)
  matrix products  184 us (17%)
  other arithmetic  77.1 us (7%)
  blocking collectives  50.1 us (5%)
  local copies, waits for them, and re-layouts  24.6 us (2%)
  between operations  15.3 us (1%)
    psum x1, waiting for transfers between devices, on_device(): lax.psum(attn_terms[1].astype(jnp.bfloat16), 'ctx').astype(jnp.float32)  184 us
    reduce_scatter x1, waiting for transfers between devices, on_device(): lax.psum_scatter(grad_values_all.astype(jnp.bfloat16), 'ctx', scatter_dim...  149 us
    all_gather x1, waiting for transfers between devices, on_device(): lax.all_gather(shaped(keys), 'ctx', axis=1, tiled=True)  96.6 us
    reduce_scatter x1, waiting for transfers between devices, on_device(): lax.psum_scatter(grad_keys_all.astype(jnp.bfloat16), 'ctx', scatter_dimen...  95.9 us
    dot_general x21, matrix products, product(): return jnp.dot(left, right, preferred_element_type=jnp.float32)  52.2 us
    psum x1, blocking collectives, on_device(): lax.psum(attn_terms[0].astype(jnp.bfloat16), 'ctx').astype(jnp.float32)  43.9 us
    all_gather x1, waiting for transfers between devices, on_device(): lax.all_gather(shaped(values), 'ctx', axis=1, tiled=True)  43.5 us
    convert_element_type x1, other arithmetic, back_core(): grad_score = (probs * (grad_prob - delta[..., None])).astype(jnp.bfloat16)  40.2 us
  transfers between devices with their start and end apart: 19, of which 17 were waited for; matrix products, arithmetic and copies ran while one was open for 16% of the time, Pallas kernels for 0%

commit v1 on v0

--- a/solution.py
+++ b/solution.py
@@ -6,6 +6,18 @@
 HEADS = 12
 HEAD_DIM = 64
 EPS = 1e-06
+
+
+def records_test(s0, bus_axis):
+    q_next, reached = (lax.axis_size(bus_axis), lax.axis_index(bus_axis))
+    z_new, heard = (s0, 1)
+    while heard < q_next:
+        earlier = lax.ppermute(z_new, bus_axis, tuple(((ix, ix ^ heard) for ix in range(q_next))))
+        everything = jnp.concatenate([z_new, earlier], 1)
+        val = jnp.concatenate([earlier, z_new], 1)
+        z_new = jnp.where(reached & heard == 0, everything, val)
+        heard = 2 * heard
+    return z_new
 
 
 def normed(rows, gain):
@@ -113,7 +125,7 @@
     values = product(normal_one, w_value).astype(jnp.bfloat16)
     keys_all, values_all = (
         lax.all_gather(shaped(keys), "ctx", axis=1, tiled=True),
-        lax.all_gather(shaped(values), "ctx", axis=1, tiled=True),
+        records_test(shaped(values), "ctx"),
     )
     mixed, logsum = lax.map(attend, (shaped(query), keys_all, values_all))
     mixed_rows = mixed.reshape(rows, width)

time: 1060 us -> 1140 us (1.075)
  waiting for transfers between devices: 697 us -> 764 us
  other arithmetic: 77.1 us -> 92.6 us
    ppermute x0 -> x4, waiting for transfers between devices: none -> 228 us  [records_test(): lax.ppermute(z_new, bus_axis, tuple(((ix, ix ^ heard) for ix in range(q_n...]
    all_gather x1, waiting for transfers between devices: 96.6 us -> 0.01 us  [on_device(): lax.all_gather(shaped(keys), 'ctx', axis=1, tiled=True)]
    all_gather x1 -> x0, waiting for transfers between devices: 43.5 us -> none  [on_device(): lax.all_gather(shaped(values), 'ctx', axis=1, tiled=True)]
    select_n x0 -> x7, other arithmetic: none -> 13.4 us  [records_test(): z_new = jnp.where(reached & heard == 0, everything, val)]
  transfers between devices with their start and end apart: 19 -> 22, of which waited for: 17 -> 16; matrix products, arithmetic and copies ran while one was open for 16% -> 16% of each run, Pallas kernels for 0% -> 0%
where the time goes in v1:
time: 1140 us
  waiting for transfers between devices  764 us (67%)
  matrix products  183 us (16%)
  other arithmetic  92.6 us (8%)
  blocking collectives  50.1 us (4%)
  local copies, waits for them, and re-layouts  27 us (2%)
  between operations  15.7 us (1%)
    ppermute x4, waiting for transfers between devices, records_test(): lax.ppermute(z_new, bus_axis, tuple(((ix, ix ^ heard) for ix in range(q_n...  228 us
    psum x1, waiting for transfers between devices, on_device(): lax.psum(attn_terms[1].astype(jnp.bfloat16), 'ctx').astype(jnp.float32)  184 us
    reduce_scatter x1, waiting for transfers between devices, on_device(): lax.psum_scatter(grad_values_all.astype(jnp.bfloat16), 'ctx', scatter_dim...  148 us
    reduce_scatter x1, waiting for transfers between devices, on_device(): lax.psum_scatter(grad_keys_all.astype(jnp.bfloat16), 'ctx', scatter_dimen...  94.1 us
    dot_general x21, matrix products, product(): return jnp.dot(left, right, preferred_element_type=jnp.float32)  50.5 us
    psum x1, blocking collectives, on_device(): lax.psum(attn_terms[0].astype(jnp.bfloat16), 'ctx').astype(jnp.float32)  43.9 us
    convert_element_type x1, other arithmetic, back_core(): grad_score = (probs * (grad_prob - delta[..., None])).astype(jnp.bfloat16)  40.1 us
    dot_general x1, matrix products, back_core(): jnp.einsum('qhd,khd->hqk', heads_of(grad_mix), heads_of(values), preferre...  39.9 us
  transfers between devices with their start and end apart: 22, of which 16 were waited for; matrix products, arithmetic and copies ran while one was open for 16% of the time, Pallas kernels for 0%

profile of v1, /device:TPU:0, one launch (start us, length us, event | category | flops | bytes accessed | tf_op | source)
XLA Modules:
  0.0 1138.8 jit_solution(1294863059677519377)
XLA Ops:
  10.1 1.9 all-gather.1
  13.3 8.2 all-gather.16.cloned.1.call-done
  21.5 2.7 convolution_convert_fusion.8
  25.4 8.1 all-gather.12.cloned.1.call-done
  37.1 9.6 collective-permute-done
  49.1 19.7 %collective-permute-done.1 = bf16[1,512,768]{2,1,0:T(8,128)(2,1)S(1)} collective-permute-done((bf16[1,512,768]{2,1,0:T(8,128)(2,1)S(1)}, bf16[1,512,768]{2,1,0:T(8,128)(2,1)S(1)}, u32[]{:S(2)}, u32[]{:S(2)}) %collective-permute-start.1) | collective-permute-done | bytes 786464 | tf_op jit(solution)/shard_map/ppermute | solution.py:15
  73.2 52.8 %collective-permute-done.2 = bf16[1,1024,768]{2,1,0:T(8,128)(2,1)S(1)} collective-permute-done((bf16[1,1024,768]{2,1,0:T(8,128)(2,1)}, bf16[1,1024,768]{2,1,0:T(8,128)(2,1)S(1)}, u32[]{:S(2)}, u32[]{:S(2)}) %collective-permute-start.2) | collective-permute-done | bytes 1572896 | tf_op jit(solution)/shard_map/ppermute | solution.py:15
  126.0 2.1 maximum_select_fusion.2
  138.2 3.0 maximum_select_fusion.3
  141.3 2.1 copy.49
  143.4 4.2 maximum_select_fusion.1
  147.6 145.9 %collective-permute-done.3 = bf16[1,2048,768]{2,1,0:T(8,128)(2,1)} collective-permute-done((bf16[1,2048,768]{2,1,0:T(8,128)(2,1)}, bf16[1,2048,768]{2,1,0:T(8,128)(2,1)}, u32[]{:S(2)}, u32[]{:S(2)}) %collective-permute-start.3) | collective-permute-done | bytes 3145760 | tf_op jit(solution)/shard_map/ppermute | solution.py:15
  293.5 4.6 copy.50
  298.1 8.7 copy.52
  306.8 21.4 %multiply_reduce_fusion.1 = (f32[12,256]{1,0:T(8,128)S(1)}, f32[12,256,4096]{2,1,0:T(8,128)}) fusion(bf16[256,12,64]{0,2,1:T(8,128)(2,1)} %bitcast.136, bf16[4096,12,64]{0,2,1:T(8,128)(2,1)} %bitcast.127), kind=kOutput, calls=%fused_computation.6 | convolution fusion | flops 1635775488 | bytes 57028608 | tf_op jit(solution)/shard_map/while/body/eval_jaxpr/qhd,khd->hqk/dot_general | solution.py:36
  328.2 20.7 %fusion = f32[12,256]{1,0:T(8,128)S(1)} fusion(f32[12,256,4096]{2,1,0:T(8,128)} %get-tuple-element.75, f32[12,256]{1,0:T(8,128)S(1)} %get-tuple-element.74), kind=kLoop, calls=%fused_computation.5 | loop fusion | flops 37745664 | bytes 50356224 | tf_op jit(solution)/shard_map/while/body/eval_jaxpr/reduce_sum | solution.py:46
  349.5 19.6 %fusion.20 = bf16[12,64,256]{2,1,0:T(8,128)(2,1)} fusion(f32[12,256,4096]{2,1,0:T(8,128)} %get-tuple-element.75, f32[12,256]{1,0:T(8,128)S(1)} %fusion, f32[12,256]{1,0:T(8,128)S(1)} %get-tuple-element.74, bf16[2048,12,64]{0,2,1:T(8,128)(2,1)S(1)} %bitcast.132, bf16[2048,12,64]{0,2,1:T(8,128)(2,1)S(1)} %maximum_select_fusion.1, pred[]{:T(512)S(6)} %eq.12), kind=kOutput, calls=%fused_computation.52 | convolution fusion | flops 1689452544 | bytes 57040896 | tf_op jit(solution)/shard_map/while/body/eval_jaxpr/hqk,khd->qhd/dot_general | solution.py:48
  369.1 2.0 multiply_reduce_fusion.4
  372.6 4.2 fusion.61
  376.8 4.3 fusion.62
  381.1 6.7 multiply_convert_fusion.2
  392.7 39.9 %multiply_reduce_fusion = (f32[12,256]{1,0:T(8,128)S(1)}, f32[12,256,4096]{2,1,0:T(8,128)}) fusion(f32[12,256,4096]{2,1,0:T(8,128)} %get-tuple-element.75, f32[12,256]{1,0:T(8,128)S(1)} %log_add_fusion, bf16[256,12,64]{0,2,1:T(8,128)(2,1)S(1)} %bitcast.140, bf16[2048,12,64]{0,2,1:T(8,128)(2,1)} %bitcast.131, bf16[2048,12,64]{0,2,1:T(8,128)(2,1)} %copy-done.2, ...), kind=kOutput, calls=%fused_computation.1 | convolution fusion | flops 1689252864 | bytes 107372544 | tf_op jit(solution)/shard_map/while/body/eval_jaxpr/qhd,khd->hqk/dot_general | solution.py:55
  432.5 40.1 %multiply_convert_fusion = bf16[12,256,4096]{2,1,0:T(8,128)(2,1)} fusion(f32[12,256,4096]{2,1,0:T(8,128)} %get-tuple-element.80, f32[12,256,4096]{2,1,0:T(8,128)} %get-tuple-element.75, f32[12,256]{1,0:T(8,128)S(1)} %get-tuple-element.79, f32[12,256]{1,0:T(8,128)S(1)} %log_add_fusion), kind=kLoop, calls=%fused_computation | loop fusion | flops 62914560 | bytes 125853696 | tf_op jit(solution)/shard_map/while/body/eval_jaxpr/convert_element_type | solution.py:59
  472.6 15.2 %multiply_convert_fusion.1 = bf16[12,64,4096]{2,1,0:T(8,128)(2,1)} fusion(bf16[256,12,64]{0,2,1:T(8,128)(2,1)S(1)} %bitcast.137, bf16[12,256,4096]{2,1,0:T(8,128)(2,1)} %multiply_convert_fusion), kind=kOutput, calls=%fused_computation.12 | convolution fusion | flops 1616904192 | bytes 31850496 | tf_op jit(solution)/shard_map/while/body/eval_jaxpr/hqk,qhd->khd/dot_general | solution.py:74
  487.9 22.1 %fusion.7 = bf16[12,64,4096]{2,1,0:T(8,128)(2,1)} fusion(bf16[256,12,64]{0,2,1:T(8,128)(2,1)S(1)} %bitcast.141, f32[12,256,4096]{2,1,0:T(8,128)} %get-tuple-element.75, f32[12,256]{1,0:T(8,128)S(1)} %log_add_fusion), kind=kOutput, calls=%fused_computation.13 | convolution fusion | flops 1651507200 | bytes 57028608 | tf_op jit(solution)/shard_map/while/body/eval_jaxpr/hqk,qhd->khd/dot_general | solution.py:77
  510.1 14.4 %fusion.19 = bf16[12,64,256]{2,1,0:T(8,128)(2,1)S(1)} fusion(bf16[4096,12,64]{0,2,1:T(8,128)(2,1)} %bitcast.128, bf16[12,256,4096]{2,1,0:T(8,128)(2,1)} %multiply_convert_fusion), kind=kOutput, calls=%fused_computation.51 | convolution fusion | flops 1611005952 | bytes 31850496 | tf_op jit(solution)/shard_map/while/body/eval_jaxpr/hqk,khd->qhd/dot_general | solution.py:64
  527.8 3.9 convolution_convert_fusion.2
  533.0 2.7 convolution_convert_fusion.1
  537.0 2.7 convolution_convert_fusion
  539.8 94.1 %reduce-scatter.10.cloned.1.call-done = bf16[1,256,768]{1,2,0:T(8,128)(2,1)} async-done(((bf16[1,4096,768]{1,2,0:T(8,128)(2,1)}), bf16[1,256,768]{1,2,0:T(8,128)(2,1)}) %reduce-scatter.10.cloned.1.call-update) | async-done | bytes 393232 | tf_op jit(solution)/shard_map/reduce_scatter | solution.py:201
  633.9 2.6 convolution_convert_fusion.5
  636.6 148.3 %reduce-scatter.12.cloned.1.call-done = bf16[1,256,768]{1,2,0:T(8,128)(2,1)} async-done(((bf16[1,4096,768]{1,2,0:T(8,128)(2,1)}), bf16[1,256,768]{1,2,0:T(8,128)(2,1)}) %reduce-scatter.12.cloned.1.call-update) | async-done | bytes 393232 | tf_op jit(solution)/shard_map/reduce_scatter | solution.py:204
  784.8 2.6 convolution_convert_fusion.4
  787.8 7.7 reduce-scatter.14.cloned.1.call-done
  795.5 12.6 %reduce-scatter.20.cloned.1.call-done = bf16[384,768]{1,0:T(8,128)(2,1)} async-done(((bf16[768,768]{1,0:T(8,128)(2,1)}), bf16[384,768]{1,0:T(8,128)(2,1)}) %reduce-scatter.20.cloned.1.call-update) | async-done | bytes 589840 | tf_op jit(solution)/shard_map/reduce_scatter | solution.py:237
  808.1 14.9 %reduce-scatter.22.cloned.1.call-done = bf16[384,2048]{1,0:T(8,128)(2,1)} async-done(((bf16[768,2048]{1,0:T(8,128)(2,1)}), bf16[384,2048]{1,0:T(8,128)(2,1)}) %reduce-scatter.22.cloned.1.call-update) | async-done | bytes 1572880 | tf_op jit(solution)/shard_map/reduce_scatter | solution.py:178
  823.1 14.8 %reduce-scatter.24.cloned.1.call-done = bf16[384,2048]{1,0:T(8,128)(2,1)} async-done(((bf16[768,2048]{1,0:T(8,128)(2,1)}), bf16[384,2048]{1,0:T(8,128)(2,1)}) %reduce-scatter.24.cloned.1.call-update) | async-done | bytes 1572880 | tf_op jit(solution)/shard_map/reduce_scatter | solution.py:181
  837.9 14.8 %reduce-scatter.26.cloned.1.call-done = bf16[1024,768]{1,0:T(8,128)(2,1)} async-done(((bf16[2048,768]{1,0:T(8,128)(2,1)}), bf16[1024,768]{1,0:T(8,128)(2,1)}) %reduce-scatter.26.cloned.1.call-update) | async-done | bytes 1572880 | tf_op jit(solution)/shard_map/reduce_scatter | solution.py:184
  852.7 12.6 %reduce-scatter.16.cloned.1.call-done = bf16[384,768]{1,0:T(8,128)(2,1)} async-done(((bf16[768,768]{1,0:T(8,128)(2,1)}), bf16[384,768]{1,0:T(8,128)(2,1)}) %reduce-scatter.16.cloned.1.call-update) | async-done | bytes 589840 | tf_op jit(solution)/shard_map/reduce_scatter | solution.py:231
  865.3 12.6 %reduce-scatter.18.cloned.1.call-done = bf16[384,768]{1,0:T(8,128)(2,1)} async-done(((bf16[768,768]{1,0:T(8,128)(2,1)}), bf16[384,768]{1,0:T(8,128)(2,1)}) %reduce-scatter.18.cloned.1.call-update) | async-done | bytes 589840 | tf_op jit(solution)/shard_map/reduce_scatter | solution.py:234
  881.6 3.8 fusion.21
  886.6 2.5 all-reduce.4
  889.2 43.9 %all-reduce.2 = (bf16[384]{0:T(512)(128)(2,1)S(1)}, bf16[384]{0:T(512)(128)(2,1)S(1)}) all-reduce(bf16[384]{0:T(512)(128)(2,1)S(1)} %dynamic-slice.3, bf16[384]{0:T(512)(128)(2,1)S(1)} %dynamic-slice.5), channel_id=1, replica_groups=mesh['dp'=2,'ctx'=16] {'ctx'}, use_global_device_ids=true, to_apply=%region_11.12 | all-reduce | flops 768 | bytes 3072 | tf_op jit(solution)/shard_map/psum | solution.py:242
  935.3 183.8 %all-reduce.7.cloned.1.call-done = (bf16[384,768]{1,0:T(8,128)(2,1)}, bf16[384,768]{1,0:T(8,128)(2,1)}, bf16[384,768]{1,0:T(8,128)(2,1)}, bf16[384,768]{1,0:T(8,...) async-done(((bf16[384,768]{1,0:T(8,128)(2,1)}, bf16[384,768]{1,0:T(8,128)(2,1)}, bf16[384,768]{1,0:T(8,128)(2,1)}, ...) | async-done | bytes 7077904 | tf_op jit(solution)/shard_map/psum | solution.py:243
  1119.1 2.3 convert_element_type.247
  1121.4 2.2 convert_element_type.249
  1125.8 2.0 convert_element_type.257
  1127.8 2.0 convert_element_type.259
  (168 shorter events, 49.7 us)
Async XLA Ops:
  7.2 14.3 %all-gather.16.cloned.1.call-start = ((), (), s32[]{:S(2)}) async-start(), calls=%async_computation.11 | async-start | bytes 1769472 | tf_op jit(solution)/shard_map/all_gather | solution.py:116
  7.9 25.6 %copy-start = (bf16[1,256,768]{2,1,0:T(8,128)(2,1)S(1)}, bf16[1,256,768]{2,1,0:T(8,128)(2,1)}, u32[]{:S(2)}) copy-start(bf16[1,256,768]{2,1,0:T(8,128)(2,1)} %param.11) | copy-start | bytes 1179652
  7.9 25.6 %all-gather.12.cloned.1.call-start = ((), (), s32[]{:S(2)}) async-start(), calls=%async_computation.9 | async-start | bytes 1769472 | tf_op jit(solution)/shard_map/all_gather | solution.py:117
  8.7 123.1 %all-gather.14.cloned.1.call-start = ((), (), s32[]{:S(2)}) async-start(), calls=%async_computation.10 | async-start | bytes 1769472 | tf_op jit(solution)/shard_map/all_gather | solution.py:115
  9.4 288.7 %all-gather.26.cloned.1.call-start = ((), (), s32[]{:S(2)}) async-start(), calls=%async_computation.25 | async-start | bytes 6684672 | tf_op jit(solution)/shard_map/all_gather | solution.py:127
  12.1 119.7 %copy-start.29 = (f32[768]{0:T(1024)}, f32[768]{0:T(1024)S(1)}, u32[]{:S(2)}) copy-start(f32[768]{0:T(1024)S(1)} %reshape.582) | copy-start | bytes 9220
  13.2 22.0 %copy-start.35 = (f32[256]{0:T(256)}, f32[256]{0:T(256)S(1)}, u32[]{:S(2)}) copy-start(f32[256]{0:T(256)S(1)} %fusion.31) | copy-start | bytes 3076
  13.3 118.6 %copy-start.33 = (f32[256]{0:T(256)}, f32[256]{0:T(256)S(1)}, u32[]{:S(2)}) copy-start(f32[256]{0:T(256)S(1)} %fusion.49) | copy-start | bytes 3076
  24.2 344.9 %all-gather.18.cloned.1.call-start = ((), (), s32[]{:S(2)}) async-start(), calls=%async_computation.12 | async-start | bytes 1769472 | tf_op jit(solution)/shard_map/all_gather | solution.py:118
  24.8 347.8 %all-gather.20.cloned.1.call-start = ((), (), s32[]{:S(2)}) async-start(), calls=%async_computation.13 | async-start | bytes 4718592 | tf_op jit(solution)/shard_map/all_gather | solution.py:135
  25.4 351.5 %all-gather.22.cloned.1.call-start = ((), (), s32[]{:S(2)}) async-start(), calls=%async_computation.14 | async-start | bytes 4718592 | tf_op jit(solution)/shard_map/all_gather | solution.py:136
  35.3 33.5 %copy-start.13 = (bf16[256,768]{1,0:T(8,128)(2,1)}, bf16[256,768]{1,0:T(8,128)(2,1)S(1)}, u32[]{:S(2)}) copy-start(bf16[256,768]{1,0:T(8,128)(2,1)S(1)} %convolution_convert_fusion.10) | copy-start | bytes 1179652
  35.3 11.4 collective-permute-start
  46.7 22.1 %copy-start.11 = (bf16[1,256,768]{2,1,0:T(8,128)(2,1)}, bf16[1,256,768]{2,1,0:T(8,128)(2,1)S(1)}, u32[]{:S(2)}) copy-start(bf16[1,256,768]{2,1,0:T(8,128)(2,1)S(1)} %collective-permute-done) | copy-start | bytes 1179652
  47.0 21.8 %collective-permute-start.1 = (bf16[1,512,768]{2,1,0:T(8,128)(2,1)S(1)}, bf16[1,512,768]{2,1,0:T(8,128)(2,1)S(1)}, u32[]{:S(2)}, u32[]{:S(2)}) collective-permute-start(bf16[1,512,768]{2,1,0:T(8,128)(2,1)S(1)} %maximum_select_fusion.9), channel_id=1, source_target_pairs={{0,2},{1,3},{2,0},{3,1},{4,6},{5,7},{6,4},{7,5},{8,10},{9,11},{10,... | collective-permute-start | bytes 2359304 | tf_op jit(solution)/shard_map/ppermute | solution.py:15
  70.6 55.4 %collective-permute-start.2 = (bf16[1,1024,768]{2,1,0:T(8,128)(2,1)}, bf16[1,1024,768]{2,1,0:T(8,128)(2,1)S(1)}, u32[]{:S(2)}, u32[]{:S(2)}) collective-permute-start(bf16[1,1024,768]{2,1,0:T(8,128)(2,1)} %maximum_select_fusion.4), channel_id=1, source_target_pairs={{0,4},{1,5},{2,6},{3,7},{4,0},{5,1},{6,2},{7,3},{8,12},{9,13},{10,... | collective-permute-start | bytes 4718600 | tf_op jit(solution)/shard_map/ppermute | solution.py:15
  72.4 308.7 %all-gather.24.cloned.1.call-start = ((), (), s32[]{:S(2)}) async-start(), calls=%async_computation.15 | async-start | bytes 4718592 | tf_op jit(solution)/shard_map/all_gather | solution.py:137
  73.1 55.3 %copy-start.37 = (bf16[384]{0:T(512)(128)(2,1)S(1)}, bf16[384]{0:T(512)(128)(2,1)}, u32[]{:S(2)}) copy-start(bf16[384]{0:T(512)(128)(2,1)} %param.18) | copy-start | bytes 2308
  73.2 57.7 %copy-start.14 = (bf16[256,768]{1,0:T(8,128)(2,1)S(1)}, bf16[256,768]{1,0:T(8,128)(2,1)}, u32[]{:S(2)}) copy-start(bf16[256,768]{1,0:T(8,128)(2,1)} %copy-done.13) | copy-start | bytes 1179652
  128.1 6.4 copy-start.12
  128.1 165.4 %collective-permute-start.3 = (bf16[1,2048,768]{2,1,0:T(8,128)(2,1)}, bf16[1,2048,768]{2,1,0:T(8,128)(2,1)}, u32[]{:S(2)}, u32[]{:S(2)}) collective-permute-start(bf16[1,2048,768]{2,1,0:T(8,128)(2,1)} %maximum_select_fusion.2), channel_id=1, source_target_pairs={{0,8},{1,9},{2,10},{3,11},{4,12},{5,13},{6,14},{7,15},{8,0},{9,1},... | collective-permute-start | bytes 9437192 | tf_op jit(solution)/shard_map/ppermute | solution.py:15
  128.4 505.5 %reduce-scatter.10.cloned.1.call-start = ((), (), s32[]{:S(2)}) async-start(), calls=%async_computation.16 | async-start | bytes 6684672 | tf_op jit(solution)/shard_map/reduce_scatter | solution.py:201
  147.6 201.3 %copy-start.2 = (bf16[2048,12,64]{0,2,1:T(8,128)(2,1)}, bf16[2048,12,64]{0,2,1:T(8,128)(2,1)S(1)}, u32[]{:S(2)}) copy-start(bf16[2048,12,64]{0,2,1:T(8,128)(2,1)S(1)} %maximum_select_fusion.1) | copy-start | bytes 9437188
  328.2 21.3 %copy-start.3 = (bf16[1,2048,768]{1,2,0:T(8,128)(2,1)S(1)}, bf16[1,2048,768]{1,2,0:T(8,128)(2,1)}, u32[]{:S(2)}) copy-start(bf16[1,2048,768]{1,2,0:T(8,128)(2,1)} %copy.50) | copy-start | bytes 9437188
  376.8 4.3 copy-start.16
  381.1 6.7 copy-start.15
  387.8 3.8 copy-start.6
  387.8 3.9 copy-start.26
  432.5 40.1 %copy-start.5 = (bf16[256,768]{0,1:T(8,128)(2,1)S(1)}, bf16[256,768]{0,1:T(8,128)(2,1)}, u32[]{:S(2)}) copy-start(bf16[256,768]{0,1:T(8,128)(2,1)} %copy.51) | copy-start | bytes 1179652
  487.9 296.9 %reduce-scatter.12.cloned.1.call-start = ((), (), s32[]{:S(2)}) async-start(), calls=%async_computation.17 | async-start | bytes 6684672 | tf_op jit(solution)/shard_map/reduce_scatter | solution.py:204
  510.1 14.5 %copy-start.30 = (f32[768]{0:T(1024)S(1)}, f32[768]{0:T(1024)}, u32[]{:S(2)}) copy-start(f32[768]{0:T(1024)} %copy-done.29) | copy-start | bytes 9220
  510.1 14.5 %copy-start.34 = (f32[256]{0:T(256)S(1)}, f32[256]{0:T(256)}, u32[]{:S(2)}) copy-start(f32[256]{0:T(256)} %copy-done.33) | copy-start | bytes 3076
  510.1 285.4 %reduce-scatter.14.cloned.1.call-start = ((), (), s32[]{:S(2)}) async-start(), calls=%async_computation.18 | async-start | bytes 1769472 | tf_op jit(solution)/shard_map/reduce_scatter | solution.py:228
  526.2 281.9 %reduce-scatter.20.cloned.1.call-start = ((), (), s32[]{:S(2)}) async-start(), calls=%async_computation.21 | async-start | bytes 1769472 | tf_op jit(solution)/shard_map/reduce_scatter | solution.py:237
  527.8 295.3 %reduce-scatter.22.cloned.1.call-start = ((), (), s32[]{:S(2)}) async-start(), calls=%async_computation.22 | async-start | bytes 4718592 | tf_op jit(solution)/shard_map/reduce_scatter | solution.py:178
  531.8 306.2 %reduce-scatter.24.cloned.1.call-start = ((), (), s32[]{:S(2)}) async-start(), calls=%async_computation.23 | async-start | bytes 4718592 | tf_op jit(solution)/shard_map/reduce_scatter | solution.py:181
  535.7 317.0 %reduce-scatter.26.cloned.1.call-start = ((), (), s32[]{:S(2)}) async-start(), calls=%async_computation.24 | async-start | bytes 4718592 | tf_op jit(solution)/shard_map/reduce_scatter | solution.py:184
  539.7 325.6 %reduce-scatter.16.cloned.1.call-start = ((), (), s32[]{:S(2)}) async-start(), calls=%async_computation.19 | async-start | bytes 1769472 | tf_op jit(solution)/shard_map/reduce_scatter | solution.py:231
  636.5 241.3 %reduce-scatter.18.cloned.1.call-start = ((), (), s32[]{:S(2)}) async-start(), calls=%async_computation.20 | async-start | bytes 1769472 | tf_op jit(solution)/shard_map/reduce_scatter | solution.py:234
  787.5 331.6 %all-reduce.7.cloned.1.call-start = ((), (), s32[]{:S(2)}) async-start(), calls=%async_computation.26 | async-start | bytes 14155776 | tf_op jit(solution)/shard_map/psum | solution.py:243
  881.6 3.8 copy-start.18
  881.6 3.8 copy-start.24
  881.6 4.3 copy-start.19
  881.6 4.3 copy-start.25
  885.4 48.9 %copy-start.36 = (f32[256]{0:T(256)S(1)}, f32[256]{0:T(256)}, u32[]{:S(2)}) copy-start(f32[256]{0:T(256)} %copy-done.35) | copy-start | bytes 3076
  1119.1 4.5 copy-start.28
  1119.1 5.6 copy-start.27
  1119.1 6.7 copy-start.23
  (13 other events, 23.9 us)
Sparse Core Ops, SparseCore 0:
  9.6 11.9 all-gather.15
  23.1 10.3 all-gather.11
  35.0 10.3 all-gather.13
  48.7 192.2 all-gather.25
  242.4 8.7 all-gather.17
  252.6 13.2 all-gather.19
  267.5 13.2 all-gather.21
  282.4 13.2 all-gather.23
  488.0 145.8 reduce-scatter.9
  639.0 145.8 reduce-scatter.11
  787.7 7.7 reduce-scatter.13
  798.3 9.8 reduce-scatter.19
  811.0 12.0 reduce-scatter.21
  825.9 12.0 reduce-scatter.23
  840.6 12.0 reduce-scatter.25
  855.5 9.8 reduce-scatter.15
  868.0 9.8 reduce-scatter.17
  885.3 233.7 all-reduce.6
